TPU v7x, 256 devices: a whole 4x4x8 slice. The times are simulated.
256 devices in a mesh: row: 16 (over z_lo, y), col: 16 (over z_hi, x, core).
Axes of the slice: x: 4, y: 4, z: 8 (z_hi: 2, z_lo: 4; z = z_hi * 4 + z_lo), core: 2. Of those that a mesh axis runs over, the one named last changes fastest.
Arguments:
- object_field: float32 [2, 2048, 2048], P(None, 'row', 'col'), may hold values from -5 to 5
- probe: float32 [2, 2, 256, 256], replicated, may hold values from -5 to 5
- amplitudes: float32 [16, 16, 2, 256, 256], P('row', 'col'), may hold values from 0.2 to 2.5
- offsets: int32 [16, 16, 2, 2], P('row', 'col'), may hold values from -128 to 0
Outputs:
- object_out: float32 [2, 2048, 2048], P(None, 'row', 'col')
- probe_out: float32 [2, 2, 256, 256], replicated
Inputs may be any that keep to these rules, and one draw needn't show every extreme that they name: `offsets`: each scan's 256 x 256 window starts at this offset from its own tile's anchor, so it reaches at most 128 pixels into neighbouring tiles.
All inputs are finite; a program needn't handle non-finite values.
Results may differ from a plain program's by a relative error of at most 0.0003.
Values sent between devices are 32-bit elements; how exact they have to be, the bound alone decides.
No kernel may reach another device: no remote copies, remote signals or barrier semaphores. Data moves between devices by JAX's collectives and lax.ppermute only.
A program may use at most 128 MiB of HBM per device.

v0:
```python
import math
import jax
import jax.numpy as jnp
from jax import lax
from jax.sharding import PartitionSpec as P

ITERS = 2
FLOOR = 0.5
OBJECT_STEP = 0.5
OBJECT_REG = 0.5
PROBE_STEP = 1.0
PROBE_REG = 1.0
HIGHEST = lax.Precision.HIGHEST


def padded_2(cells, sides, width):
    for axis, dim in sides:
        count = lax.axis_size(axis)
        ends = count - 1
        head = lax.slice_in_dim(cells, 0, width, axis=dim)
        tail = lax.slice_in_dim(cells, cells.shape[dim] - width, cells.shape[dim], axis=dim)
        cells = jnp.concatenate(
            [
                lax.ppermute(tail, axis, [(i, (i + 1) % count) for i in range(ends)]),
                cells,
                lax.ppermute(head, axis, [((i + 1) % count, i) for i in range(ends)]),
            ],
            axis=dim,
        )
    return cells


def tables(side):
    indices = lax.iota(jnp.int32, side)
    phases = indices[:, None] * indices[None, :] % side
    angles = phases.astype(jnp.float32) * (2.0 * math.pi / side)
    scaling = 1.0 / math.sqrt(side)
    return (jnp.cos(angles) * scaling, jnp.sin(angles) * scaling)


def last_axis(real_part, imag_part, cos_table, sin_table):
    product_one = jnp.matmul(real_part, cos_table, precision=HIGHEST)
    product_two = jnp.matmul(imag_part, sin_table, precision=HIGHEST)
    product_three = jnp.matmul(real_part + imag_part, cos_table + sin_table, precision=HIGHEST)
    return (product_one - product_two, product_three - product_one - product_two)


def first_axis(real_part, imag_part, cos_table, sin_table):
    product_one = jnp.einsum("jk,bkl->bjl", cos_table, real_part, precision=HIGHEST)
    product_two = jnp.einsum("jk,bkl->bjl", sin_table, imag_part, precision=HIGHEST)
    product_three = jnp.einsum(
        "jk,bkl->bjl", cos_table + sin_table, real_part + imag_part, precision=HIGHEST
    )
    return (product_one - product_two, product_three - product_one - product_two)


def transform(real_part, imag_part, cos_table, sin_table):
    real_part, imag_part = last_axis(real_part, imag_part, cos_table, sin_table)
    return first_axis(real_part, imag_part, cos_table, sin_table)


def fold_axis(extended, axis_number, tile_side, half_width):
    own_part = lax.slice_in_dim(
        extended, 2 * half_width, 2 * half_width + tile_side, axis=axis_number
    )
    low_rim = lax.slice_in_dim(extended, 0, half_width, axis=axis_number)
    high_rim = lax.slice_in_dim(
        extended, tile_side + 3 * half_width, tile_side + 4 * half_width, axis=axis_number
    )
    low_widths = [(0, 0)] * extended.ndim
    high_widths = [(0, 0)] * extended.ndim
    low_widths[axis_number] = (0, tile_side - half_width)
    high_widths[axis_number] = (tile_side - half_width, 0)
    return own_part + low_rim + high_rim


def cut_windows(padded, starts, probe_side):
    zero_index = jnp.zeros((), jnp.int32)

    def cut_one(corner):
        return lax.dynamic_slice(
            padded, (zero_index, corner[0], corner[1]), (padded.shape[0], probe_side, probe_side)
        )

    return jax.vmap(cut_one)(starts)


def local(object_field, probe, amplitudes, offsets):
    tile_side = object_field.shape[1]
    mode_count = probe.shape[1]
    probe_side = probe.shape[2]
    half_width = probe_side // 2
    starts = offsets[0, 0] + half_width
    measured = amplitudes[0, 0]
    scan_count = starts.shape[0]
    zero_index = jnp.zeros((), jnp.int32)
    cos_table, sin_table = tables(probe_side)
    padded = padded_2(object_field, (("row", 1), ("col", 2)), half_width)
    for iteration in range(ITERS):
        windows = cut_windows(padded, starts, probe_side)
        win_real = windows[:, 0][:, None]
        win_imag = windows[:, 1][:, None]
        probe_real = probe[0][None]
        probe_imag = probe[1][None]
        exit_real = (probe_real * win_real - probe_imag * win_imag).reshape(
            -1, probe_side, probe_side
        )
        exit_imag = (probe_real * win_imag + probe_imag * win_real).reshape(
            -1, probe_side, probe_side
        )
        far_real, far_imag = transform(exit_real, exit_imag, cos_table, -sin_table)
        far_real = far_real.reshape(scan_count, mode_count, probe_side, probe_side)
        far_imag = far_imag.reshape(scan_count, mode_count, probe_side, probe_side)
        intensity = jnp.sum(far_real * far_real + far_imag * far_imag, axis=1)
        factor = (measured / jnp.maximum(jnp.sqrt(intensity), FLOOR) - 1.0)[:, None]
        back_real, back_imag = transform(
            (far_real * factor).reshape(-1, probe_side, probe_side),
            (far_imag * factor).reshape(-1, probe_side, probe_side),
            cos_table,
            sin_table,
        )
        back_real = back_real.reshape(scan_count, mode_count, probe_side, probe_side)
        back_imag = back_imag.reshape(scan_count, mode_count, probe_side, probe_side)
        obj_real = jnp.sum(probe_real * back_real + probe_imag * back_imag, axis=1)
        obj_imag = jnp.sum(probe_real * back_imag - probe_imag * back_real, axis=1)
        probe_power = jnp.sum(probe[0] * probe[0] + probe[1] * probe[1], axis=0)
        grad_probe = jnp.stack(
            [
                jnp.sum(win_real * back_real + win_imag * back_imag, axis=0),
                jnp.sum(win_real * back_imag - win_imag * back_real, axis=0),
            ]
        )
        probe_weight = jnp.sum(
            windows[:, 0] * windows[:, 0] + windows[:, 1] * windows[:, 1], axis=0
        )
        channels = 3
        gradient = jnp.zeros(
            (channels, tile_side + 2 * half_width, tile_side + 2 * half_width), jnp.float32
        )
        for scan_index in range(scan_count):
            contrib = jnp.stack([obj_real[scan_index], obj_imag[scan_index], probe_power])
            corner = (zero_index, starts[scan_index, 0], starts[scan_index, 1])
            gradient = lax.dynamic_update_slice(
                gradient, lax.dynamic_slice(gradient, corner, contrib.shape) + contrib, corner
            )
        extended = padded_2(gradient, (("row", 1), ("col", 2)), half_width)
        totals = fold_axis(fold_axis(extended, 1, tile_side, half_width), 2, tile_side, half_width)
        summed_grad, summed_weight = lax.psum((grad_probe, probe_weight), ("row", "col"))
        new_probe = probe + PROBE_STEP * summed_grad / (summed_weight + PROBE_REG)
        object_field = object_field + OBJECT_STEP * totals[0:2] / (totals[2:3] + OBJECT_REG)
        if iteration + 1 < ITERS:
            padded = padded_2(object_field, (("row", 1), ("col", 2)), half_width)
        probe = new_probe
    return (object_field, probe)


def solution(mesh):
    return jax.shard_map(
        local,
        mesh=mesh,
        in_specs=(
            P(None, "row", "col"),
            P(),
            P("row", "col", None, None, None),
            P("row", "col", None, None),
        ),
        out_specs=(P(None, "row", "col"), P()),
        check_vma=False,
    )
```

profile of v0, /device:TPU:2, one launch (start us, length us, event | category | flops | bytes accessed | tf_op | source)
XLA Modules:
  0.0 828.7 jit_solution(15070879831426267204)
XLA Ops:
  7.2 3.6 collective-permute-start
  19.9 3.6 collective-permute-start.3
  36.4 4.3 while.2
  49.5 3.9 fusion.53
  72.7 13.8 %fusion.10 = f32[4,256,256]{2,1,0:T(8,128)S(1)} fusion(f32[4,256,256]{2,1,0:T(8,128)S(1)} %fusion.43, f32[4,256,256]{2,1,0:T(8,128)S(1)} %fusion.62, f32[4,256,256]{1,2,0:T(8,128)S(1)} %get-tuple-element.94, f32[4,256,256]{1,2,0:T(8,128)S(1)} %get-tuple-element.95), kind=kOutput, calls=%fused_computation.34 | convolution fusion | flops 807206912 | bytes 5242880 | tf_op jit(solution)/shard_map/dot_general | solution.py:44
  91.9 4.6 add_reduce_fusion.3
  98.3 10.7 %dynamic_update_slice.12 = f32[3,384,384]{1,2,0:T(8,128)S(1)} dynamic-update-slice(f32[3,384,384]{1,2,0:T(8,128)S(1)} %broadcast.83.clone, f32[3,256,256]{1,2,0:T(8,128)} %pad_maximum_fusion.5, s32[]{:T(128)} %constant.12.clone.1, s32[]{:T(128)S(6)} %select_n.86, s32[]{:T(128)S(6)} %select_n.87) | dynamic-update-slice | bytes 1572868 | tf_op jit(solution)/shard_map/dynamic_update_slice | solution.py:143
  111.0 11.3 %dynamic_update_slice.13 = f32[3,384,384]{1,2,0:T(8,128)S(1)} dynamic-update-slice(f32[3,384,384]{1,2,0:T(8,128)S(1)} %dynamic_update_slice.12, f32[3,256,256]{1,2,0:T(8,128)} %fusion.21, s32[]{:T(128)} %constant.12.clone.1, s32[]{:T(128)S(6)} %select_n.88, s32[]{:T(128)S(6)} %select_n.89) | dynamic-update-slice | bytes 1572868 | tf_op jit(solution)/shard_map/dynamic_update_slice | solution.py:143
  129.2 8.5 %collective-permute-done.4 = f32[3,128,384]{1,2,0:T(8,128)S(1)} collective-permute-done((f32[3,128,384]{1,2,0:T(8,128)S(1)}, f32[3,128,384]{1,2,0:T(8,128)S(1)}, u32[]{:S(2)}, u32[]{:S(2)}) %collective-permute-start.4) | collective-permute-done | bytes 589856 | tf_op jit(solution)/shard_map/ppermute | solution.py:24
  137.6 4.8 collective-permute-done.5
  145.9 3.6 collective-permute-start.7
  153.5 265.9 %all-reduce.7.cloned.1.call-done = (f32[2,2,256,256]{2,3,1,0:T(8,128)}, f32[256,256]{1,0:T(8,128)}) async-done(((f32[2,2,256,256]{2,3,1,0:T(8,128)}, f32[256,256]{1,0:T(8,128)}), (f32[2,2,256,256]{2,3,1,0:T(8,128)}, f32[256,256]{1,0:T(8,128)})) %all-reduce.7.cloned.1.call-update) | async-done | bytes 1310736 | tf_op jit(solution)/shard_map/psum | solution.py:148
  428.5 4.4 collective-permute-done.9
  434.8 3.6 collective-permute-start.11
  444.9 7.5 while.3
  458.6 3.9 fusion.50
  483.2 3.0 fusion.8
  491.6 4.5 add_reduce_fusion.1
  498.0 10.7 %dynamic_update_slice.14 = f32[3,384,384]{1,2,0:T(8,128)S(1)} dynamic-update-slice(f32[3,384,384]{1,2,0:T(8,128)S(1)} %broadcast.83, f32[3,256,256]{1,2,0:T(8,128)} %pad_maximum_fusion.7, s32[]{:T(128)} %constant.12.clone.1, s32[]{:T(128)S(6)} %select_n.86, s32[]{:T(128)S(6)} %select_n.87) | dynamic-update-slice | bytes 1572868 | tf_op jit(solution)/shard_map/dynamic_update_slice | solution.py:143
  510.8 11.6 %dynamic_update_slice.15 = f32[3,384,384]{1,2,0:T(8,128)S(1)} dynamic-update-slice(f32[3,384,384]{1,2,0:T(8,128)S(1)} %dynamic_update_slice.14, f32[3,256,256]{1,2,0:T(8,128)} %fusion.20, s32[]{:T(128)} %constant.12.clone.1, s32[]{:T(128)S(6)} %select_n.88, s32[]{:T(128)S(6)} %select_n.89) | dynamic-update-slice | bytes 1572868 | tf_op jit(solution)/shard_map/dynamic_update_slice | solution.py:143
  531.5 8.1 collective-permute-done.12
  539.6 4.2 collective-permute-done.13
  548.6 3.2 collective-permute-start.15
  551.8 258.8 %all-reduce.5.cloned.1.call-done = (f32[2,2,256,256]{2,3,1,0:T(8,128)}, f32[256,256]{1,0:T(8,128)}) async-done(((f32[2,2,256,256]{2,3,1,0:T(8,128)}, f32[256,256]{1,0:T(8,128)}), (f32[2,2,256,256]{2,3,1,0:T(8,128)}, f32[256,256]{1,0:T(8,128)})) %all-reduce.5.cloned.1.call-update) | async-done | bytes 1310736 | tf_op jit(solution)/shard_map/psum | solution.py:148
  (198 shorter events, 154.8 us)
Async XLA Ops:
  7.2 7.0 copy-start
  7.2 412.3 %all-reduce.7.cloned.1.call-start = ((), (), s32[]{:S(2)}) async-start(), calls=%async_computation.1 | async-start | bytes 2621440 | tf_op jit(solution)/shard_map/psum | solution.py:148
  7.2 7.0 collective-permute-start
  10.8 7.1 collective-permute-start.1
  15.0 16.1 %copy-start.29 = (f32[1,1,2,256,256]{4,3,2,1,0:T(8,128)S(1)}, f32[1,1,2,256,256]{4,3,2,1,0:T(8,128)}, u32[]{:S(2)}) copy-start(f32[1,1,2,256,256]{4,3,2,1,0:T(8,128)} %param.6) | copy-start | bytes 1572868
  17.9 14.2 %copy-start.27 = (f32[2,384,128]{2,1,0:T(8,128)}, f32[2,384,128]{2,1,0:T(8,128)S(1)}, u32[]{:S(2)}) copy-start(f32[2,384,128]{2,1,0:T(8,128)S(1)} %constant_dynamic-update-slice_fusion) | copy-start | bytes 1179652
  18.0 17.0 %collective-permute-start.2 = (f32[2,384,128]{2,1,0:T(8,128)S(1)}, f32[2,384,128]{2,1,0:T(8,128)}, u32[]{:S(2)}, u32[]{:S(2)}) collective-permute-start(f32[2,384,128]{2,1,0:T(8,128)S(1)} %constant_dynamic-update-slice_fusion), channel_id=1, source_target_pairs={{0,1},{1,2},{2,3},{3,4},{4,5},{5,6},{6,7},{7,8},{8,9},{9,10},{10,1... | collective-permute-start | bytes 1179656 | tf_op jit(solution)/shard_map/ppermute | solution.py:24
  19.9 15.1 %collective-permute-start.3 = (f32[2,384,128]{2,1,0:T(8,128)S(1)}, f32[2,384,128]{2,1,0:T(8,128)}, u32[]{:S(2)}, u32[]{:S(2)}) collective-permute-start(f32[2,384,128]{2,1,0:T(8,128)S(1)} %constant_dynamic-update-slice_fusion), channel_id=1, source_target_pairs={{1,0},{2,1},{3,2},{4,3},{5,4},{6,5},{7,6},{8,7},{9,8},{10,9},{11,1... | collective-permute-start | bytes 1179656 | tf_op jit(solution)/shard_map/ppermute | solution.py:26
  122.5 15.2 %collective-permute-start.4 = (f32[3,128,384]{1,2,0:T(8,128)S(1)}, f32[3,128,384]{1,2,0:T(8,128)S(1)}, u32[]{:S(2)}, u32[]{:S(2)}) collective-permute-start(f32[3,128,384]{1,2,0:T(8,128)S(1)} %get-tuple-element.78), channel_id=1, source_target_pairs={{0,16},{16,32},{32,48},{48,64},{64,80},{80,96},{96,112},{112,128},... | collective-permute-start | bytes 1769480 | tf_op jit(solution)/shard_map/ppermute | solution.py:24
  125.3 17.1 %collective-permute-start.5 = (f32[3,128,384]{1,2,0:T(8,128)S(1)}, f32[3,128,384]{1,2,0:T(8,128)S(1)}, u32[]{:S(2)}, u32[]{:S(2)}) collective-permute-start(f32[3,128,384]{1,2,0:T(8,128)S(1)} %get-tuple-element.79), channel_id=1, source_target_pairs={{16,0},{32,16},{48,32},{64,48},{80,64},{96,80},{112,96},{128,112},... | collective-permute-start | bytes 1769480 | tf_op jit(solution)/shard_map/ppermute | solution.py:26
  143.9 277.3 %collective-permute-start.6 = (f32[3,640,128]{1,2,0:T(8,128)}, f32[3,640,128]{1,2,0:T(8,128)}, u32[]{:S(2)}, u32[]{:S(2)}) collective-permute-start(f32[3,640,128]{1,2,0:T(8,128)} %get-tuple-element.70), channel_id=1, source_target_pairs={{0,1},{1,2},{2,3},{3,4},{4,5},{5,6},{6,7},{7,8},{8,9},{9,10},{10,1... | collective-permute-start | bytes 2949128 | tf_op jit(solution)/shard_map/ppermute | solution.py:24
  145.9 275.4 %collective-permute-start.7 = (f32[3,640,128]{1,2,0:T(8,128)}, f32[3,640,128]{1,2,0:T(8,128)}, u32[]{:S(2)}, u32[]{:S(2)}) collective-permute-start(f32[3,640,128]{1,2,0:T(8,128)} %get-tuple-element.71), channel_id=1, source_target_pairs={{1,0},{2,1},{3,2},{4,3},{5,4},{6,5},{7,6},{8,7},{9,8},{10,9},{11,1... | collective-permute-start | bytes 2949128 | tf_op jit(solution)/shard_map/ppermute | solution.py:26
  150.6 660.1 %all-reduce.5.cloned.1.call-start = ((), (), s32[]{:S(2)}) async-start(), calls=%async_computation | async-start | bytes 2621440 | tf_op jit(solution)/shard_map/psum | solution.py:148
  153.5 267.8 %copy-start.24 = (f32[3,128,384]{1,2,0:T(8,128)S(1)}, f32[3,128,384]{1,2,0:T(8,128)}, u32[]{:S(2)}) copy-start(f32[3,128,384]{1,2,0:T(8,128)} %copy-done.23) | copy-start | bytes 1769476
  421.3 6.0 copy-start.26
  421.3 6.0 copy-start.22
  423.0 5.5 collective-permute-start.8
  426.0 6.9 collective-permute-start.9
  432.9 9.1 %collective-permute-start.10 = (f32[2,384,128]{1,2,0:T(8,128)S(1)}, f32[2,384,128]{1,2,0:T(8,128)S(1)}, u32[]{:S(2)}, u32[]{:S(2)}) collective-permute-start(f32[2,384,128]{1,2,0:T(8,128)S(1)} %pad_maximum_fusion.14), channel_id=1, source_target_pairs={{0,1},{1,2},{2,3},{3,4},{4,5},{5,6},{6,7},{7,8},{8,9},{9,10},{10,1... | collective-permute-start | bytes 1179656 | tf_op jit(solution)/shard_map/ppermute | solution.py:24
  434.8 8.9 %collective-permute-start.11 = (f32[2,384,128]{1,2,0:T(8,128)S(1)}, f32[2,384,128]{1,2,0:T(8,128)S(1)}, u32[]{:S(2)}, u32[]{:S(2)}) collective-permute-start(f32[2,384,128]{1,2,0:T(8,128)S(1)} %pad_maximum_fusion.14), channel_id=1, source_target_pairs={{1,0},{2,1},{3,2},{4,3},{5,4},{6,5},{7,6},{8,7},{9,8},{10,9},{11,1... | collective-permute-start | bytes 1179656 | tf_op jit(solution)/shard_map/ppermute | solution.py:26
  523.5 16.1 %collective-permute-start.12 = (f32[3,128,384]{1,2,0:T(8,128)}, f32[3,128,384]{1,2,0:T(8,128)S(1)}, u32[]{:S(2)}, u32[]{:S(2)}) collective-permute-start(f32[3,128,384]{1,2,0:T(8,128)} %get-tuple-element.76), channel_id=1, source_target_pairs={{0,16},{16,32},{32,48},{48,64},{64,80},{80,96},{96,112},{112,128},... | collective-permute-start | bytes 1769480 | tf_op jit(solution)/shard_map/ppermute | solution.py:24
  526.0 17.8 %collective-permute-start.13 = (f32[3,128,384]{1,2,0:T(8,128)}, f32[3,128,384]{1,2,0:T(8,128)}, u32[]{:S(2)}, u32[]{:S(2)}) collective-permute-start(f32[3,128,384]{1,2,0:T(8,128)} %get-tuple-element.77), channel_id=1, source_target_pairs={{16,0},{32,16},{48,32},{64,48},{80,64},{96,80},{112,96},{128,112},... | collective-permute-start | bytes 1769480 | tf_op jit(solution)/shard_map/ppermute | solution.py:26
  546.3 272.8 %collective-permute-start.14 = (f32[3,640,128]{1,2,0:T(8,128)}, f32[3,640,128]{1,2,0:T(8,128)}, u32[]{:S(2)}, u32[]{:S(2)}) collective-permute-start(f32[3,640,128]{1,2,0:T(8,128)} %get-tuple-element.68), channel_id=1, source_target_pairs={{0,1},{1,2},{2,3},{3,4},{4,5},{5,6},{6,7},{7,8},{8,9},{9,10},{10,1... | collective-permute-start | bytes 2949128 | tf_op jit(solution)/shard_map/ppermute | solution.py:24
  548.6 270.5 %collective-permute-start.15 = (f32[3,640,128]{1,2,0:T(8,128)}, f32[3,640,128]{1,2,0:T(8,128)}, u32[]{:S(2)}, u32[]{:S(2)}) collective-permute-start(f32[3,640,128]{1,2,0:T(8,128)} %get-tuple-element.69), channel_id=1, source_target_pairs={{1,0},{2,1},{3,2},{4,3},{5,4},{6,5},{7,6},{8,7},{9,8},{10,9},{11,1... | collective-permute-start | bytes 2949128 | tf_op jit(solution)/shard_map/ppermute | solution.py:26
  (26 other events, 77.3 us)
Sparse Core Ops, SparseCore 0:
  150.7 268.7 all-reduce.6
  531.6 279.0 all-reduce.4
where the time goes:
time: 841 us; the launch traced here: 829 us
  waiting for transfers between devices  563 us (67%)
  local copies, waits for them, and re-layouts  86.8 us (10%)
  matrix products  82 us (10%)
  starting transfers between devices  39.3 us (5%)
  other arithmetic  34.4 us (4%)
  between operations  22.9 us (3%)
    psum x2, waiting for transfers between devices, local(): lax.psum((grad_probe, probe_weight), ('row', 'col'))  525 us
    dynamic_update_slice x4, local copies, waits for them, and re-layouts, local(): lax.dynamic_update_slice(gradient, lax.dynamic_slice(gradient, corner, co...  44.2 us
    dot_general x4, matrix products, last_axis(): jnp.matmul(real_part + imag_part, cos_table + sin_table, precision=HIGHEST)  21.1 us
    ppermute x8, waiting for transfers between devices, padded_2(): lax.ppermute(tail, axis, [(i, (i + 1) % count) for i in range(ends)])  20 us
    ppermute x8, starting transfers between devices, padded_2(): lax.ppermute(tail, axis, [(i, (i + 1) % count) for i in range(ends)])  19.9 us
    ppermute x8, starting transfers between devices, padded_2(): lax.ppermute(head, axis, [((i + 1) % count, i) for i in range(ends)])  19.3 us
    ppermute x8, waiting for transfers between devices, padded_2(): lax.ppermute(head, axis, [((i + 1) % count, i) for i in range(ends)])  17.9 us
  transfers between devices with their start and end apart: 18, of which 11 were waited for; matrix products, arithmetic and copies ran while one was open for 4% of the time, Pallas kernels for 0%

commit v1 on v0

--- a/solution.py
+++ b/solution.py
@@ -145,7 +145,7 @@
             )
         extended = padded_2(gradient, (("row", 1), ("col", 2)), half_width)
         totals = fold_axis(fold_axis(extended, 1, tile_side, half_width), 2, tile_side, half_width)
-        summed_grad, summed_weight = lax.psum((grad_probe, probe_weight), ("row", "col"))
+        summed_grad, summed_weight = lax.psum(lax.psum((grad_probe, probe_weight), "row"), "col")
         new_probe = probe + PROBE_STEP * summed_grad / (summed_weight + PROBE_REG)
         object_field = object_field + OBJECT_STEP * totals[0:2] / (totals[2:3] + OBJECT_REG)
         if iteration + 1 < ITERS:

time: 841 us -> 931 us (1.11)
  the two profiles are of different devices: /device:TPU:2 before, /device:TPU:1 now
where the time goes in v1:
time: 931 us; the launch traced here: 919 us
  waiting for transfers between devices  663 us (71%)
  matrix products  80.2 us (9%)
  local copies, waits for them, and re-layouts  78.9 us (8%)
  starting transfers between devices  47.1 us (5%)
  other arithmetic  26.1 us (3%)
  between operations  22.9 us (2%)
    psum x2, waiting for transfers between devices, local(): lax.psum(lax.psum((grad_probe, probe_weight), 'row'), 'col')  374 us
    psum x2, waiting for transfers between devices, local(): lax.psum((grad_probe, probe_weight), 'row')  238 us
    dynamic_update_slice x4, local copies, waits for them, and re-layouts, local(): lax.dynamic_update_slice(gradient, lax.dynamic_slice(gradient, corner, co...  42.6 us
    ppermute x8, starting transfers between devices, padded_2(): lax.ppermute(tail, axis, [(i, (i + 1) % count) for i in range(ends)])  32.4 us
    ppermute x8, waiting for transfers between devices, padded_2(): lax.ppermute(tail, axis, [(i, (i + 1) % count) for i in range(ends)])  30.8 us
    dot_general x4, matrix products, last_axis(): jnp.matmul(real_part + imag_part, cos_table + sin_table, precision=HIGHEST)  20.7 us
    ppermute x8, waiting for transfers between devices, padded_2(): lax.ppermute(head, axis, [((i + 1) % count, i) for i in range(ends)])  20.5 us
  transfers between devices with their start and end apart: 20, of which 13 were waited for; matrix products, arithmetic and copies ran while one was open for 5% of the time, Pallas kernels for 0%

profile of v1, /device:TPU:1, one launch (start us, length us, event | category | flops | bytes accessed | tf_op | source)
XLA Modules:
  0.0 919.2 jit_solution(3792216798255435999)
XLA Ops:
  7.2 4.2 collective-permute-start
  17.4 5.1 collective-permute-start.2
  37.5 4.0 while.2
  50.4 3.9 fusion.53
  73.5 13.4 %fusion.10 = f32[4,256,256]{2,1,0:T(8,128)S(1)} fusion(f32[4,256,256]{2,1,0:T(8,128)S(1)} %fusion.43, f32[4,256,256]{2,1,0:T(8,128)S(1)} %fusion.62, f32[4,256,256]{1,2,0:T(8,128)S(1)} %get-tuple-element.98, f32[4,256,256]{1,2,0:T(8,128)S(1)} %get-tuple-element.99), kind=kOutput, calls=%fused_computation.34 | convolution fusion | flops 807206912 | bytes 5242880 | tf_op jit(solution)/shard_map/dot_general | solution.py:44
  92.4 4.6 add_reduce_fusion.3
  98.8 10.8 %dynamic_update_slice.12 = f32[3,384,384]{1,2,0:T(8,128)S(1)} dynamic-update-slice(f32[3,384,384]{1,2,0:T(8,128)S(1)} %broadcast.83.clone, f32[3,256,256]{1,2,0:T(8,128)} %pad_maximum_fusion.5, s32[]{:T(128)} %constant.12.clone.1, s32[]{:T(128)S(6)} %select_n.86, s32[]{:T(128)S(6)} %select_n.87) | dynamic-update-slice | bytes 1572868 | tf_op jit(solution)/shard_map/dynamic_update_slice | solution.py:143
  111.7 10.3 %dynamic_update_slice.13 = f32[3,384,384]{1,2,0:T(8,128)S(1)} dynamic-update-slice(f32[3,384,384]{1,2,0:T(8,128)S(1)} %dynamic_update_slice.12, f32[3,256,256]{1,2,0:T(8,128)} %fusion.21, s32[]{:T(128)} %constant.12.clone.1, s32[]{:T(128)S(6)} %select_n.88, s32[]{:T(128)S(6)} %select_n.89) | dynamic-update-slice | bytes 1572868 | tf_op jit(solution)/shard_map/dynamic_update_slice | solution.py:143
  127.4 9.8 %collective-permute-done.4 = f32[3,128,384]{1,2,0:T(8,128)S(1)} collective-permute-done((f32[3,128,384]{1,2,0:T(8,128)S(1)}, f32[3,128,384]{1,2,0:T(8,128)S(1)}, u32[]{:S(2)}, u32[]{:S(2)}) %collective-permute-start.4) | collective-permute-done | bytes 589856 | tf_op jit(solution)/shard_map/ppermute | solution.py:24
  137.2 4.4 collective-permute-done.5
  143.2 4.9 collective-permute-start.6
  153.6 5.7 collective-permute-done.6
  159.4 4.4 collective-permute-done.7
  165.4 5.4 collective-permute-start.8
  172.7 4.7 collective-permute-done.9
  184.4 135.8 %all-reduce.15.cloned.1.call-done = (f32[2,2,256,256]{2,3,1,0:T(8,128)}, f32[256,256]{1,0:T(8,128)}) async-done(((f32[2,2,256,256]{2,3,1,0:T(8,128)}, f32[256,256]{1,0:T(8,128)}), (f32[2,2,256,256]{2,3,1,0:T(8,128)}, f32[256,256]{1,0:T(8,128)})) %all-reduce.15.cloned.1.call-update) | async-done | bytes 1310736 | tf_op jit(solution)/shard_map/psum | solution.py:148
  320.5 5.1 while.3
  328.4 184.3 %all-reduce.11.cloned.1.call-done = (f32[2,2,256,256]{2,3,1,0:T(8,128)}, f32[256,256]{1,0:T(8,128)}) async-done(((f32[2,2,256,256]{2,3,1,0:T(8,128)}, f32[256,256]{1,0:T(8,128)}), (f32[2,2,256,256]{2,3,1,0:T(8,128)}, f32[256,256]{1,0:T(8,128)})) %all-reduce.11.cloned.1.call-update) | async-done | bytes 1310736 | tf_op jit(solution)/shard_map/psum | solution.py:148
  560.0 11.1 %dynamic_update_slice.14 = f32[3,384,384]{1,2,0:T(8,128)S(1)} dynamic-update-slice(f32[3,384,384]{1,2,0:T(8,128)S(1)} %broadcast.83, f32[3,256,256]{1,2,0:T(8,128)} %pad_maximum_fusion.7, s32[]{:T(128)} %constant.12.clone.1, s32[]{:T(128)S(6)} %select_n.86, s32[]{:T(128)S(6)} %select_n.87) | dynamic-update-slice | bytes 1572868 | tf_op jit(solution)/shard_map/dynamic_update_slice | solution.py:143
  573.2 10.3 %dynamic_update_slice.15 = f32[3,384,384]{1,2,0:T(8,128)S(1)} dynamic-update-slice(f32[3,384,384]{1,2,0:T(8,128)S(1)} %dynamic_update_slice.14, f32[3,256,256]{1,2,0:T(8,128)} %fusion.20, s32[]{:T(128)} %constant.12.clone.1, s32[]{:T(128)S(6)} %select_n.88, s32[]{:T(128)S(6)} %select_n.89) | dynamic-update-slice | bytes 1572868 | tf_op jit(solution)/shard_map/dynamic_update_slice | solution.py:143
  588.5 14.7 %collective-permute-done.12 = f32[3,128,384]{1,2,0:T(8,128)S(1)} collective-permute-done((f32[3,128,384]{1,2,0:T(8,128)S(1)}, f32[3,128,384]{1,2,0:T(8,128)S(1)}, u32[]{:S(2)}, u32[]{:S(2)}) %collective-permute-start.12) | collective-permute-done | bytes 589856 | tf_op jit(solution)/shard_map/ppermute | solution.py:24
  603.2 5.2 collective-permute-done.13
  615.1 101.9 %all-reduce.13.cloned.1.call-done = (f32[2,2,256,256]{2,3,1,0:T(8,128)}, f32[256,256]{1,0:T(8,128)}) async-done(((f32[2,2,256,256]{2,3,1,0:T(8,128)}, f32[256,256]{1,0:T(8,128)}), (f32[2,2,256,256]{2,3,1,0:T(8,128)}, f32[256,256]{1,0:T(8,128)})) %all-reduce.13.cloned.1.call-update) | async-done | bytes 1310736 | tf_op jit(solution)/shard_map/psum | solution.py:148
  719.4 190.0 %all-reduce.9.cloned.1.call-done = (f32[2,2,256,256]{2,3,1,0:T(8,128)}, f32[256,256]{1,0:T(8,128)}) async-done(((f32[2,2,256,256]{2,3,1,0:T(8,128)}, f32[256,256]{1,0:T(8,128)}), (f32[2,2,256,256]{2,3,1,0:T(8,128)}, f32[256,256]{1,0:T(8,128)})) %all-reduce.9.cloned.1.call-update) | async-done | bytes 1310736 | tf_op jit(solution)/shard_map/psum | solution.py:148
  (208 shorter events, 150.6 us)
Async XLA Ops:
  7.2 313.0 %all-reduce.15.cloned.1.call-start = ((), (), s32[]{:S(2)}) async-start(), calls=%async_computation.3 | async-start | bytes 2621440 | tf_op jit(solution)/shard_map/psum | solution.py:148
  7.2 7.5 collective-permute-start
  11.4 5.9 collective-permute-start.1
  17.4 18.7 %collective-permute-start.2 = (f32[2,384,128]{2,1,0:T(8,128)S(1)}, f32[2,384,128]{2,1,0:T(8,128)}, u32[]{:S(2)}, u32[]{:S(2)}) collective-permute-start(f32[2,384,128]{2,1,0:T(8,128)S(1)} %constant_dynamic-update-slice_fusion), channel_id=1, source_target_pairs={{0,1},{1,2},{2,3},{3,4},{4,5},{5,6},{6,7},{7,8},{8,9},{9,10},{10,1... | collective-permute-start | bytes 1179656 | tf_op jit(solution)/shard_map/ppermute | solution.py:24
  22.5 13.6 %collective-permute-start.3 = (f32[2,384,128]{2,1,0:T(8,128)S(1)}, f32[2,384,128]{2,1,0:T(8,128)}, u32[]{:S(2)}, u32[]{:S(2)}) collective-permute-start(f32[2,384,128]{2,1,0:T(8,128)S(1)} %constant_dynamic-update-slice_fusion), channel_id=1, source_target_pairs={{1,0},{2,1},{3,2},{4,3},{5,4},{6,5},{7,6},{8,7},{9,8},{10,9},{11,1... | collective-permute-start | bytes 1179656 | tf_op jit(solution)/shard_map/ppermute | solution.py:26
  122.2 15.0 %collective-permute-start.4 = (f32[3,128,384]{1,2,0:T(8,128)S(1)}, f32[3,128,384]{1,2,0:T(8,128)S(1)}, u32[]{:S(2)}, u32[]{:S(2)}) collective-permute-start(f32[3,128,384]{1,2,0:T(8,128)S(1)} %get-tuple-element.82), channel_id=1, source_target_pairs={{0,16},{16,32},{32,48},{48,64},{64,80},{80,96},{96,112},{112,128},... | collective-permute-start | bytes 1769480 | tf_op jit(solution)/shard_map/ppermute | solution.py:24
  125.8 24.2 %copy-start.12 = (f32[2,256,256]{1,2,0:T(8,128)S(1)}, f32[2,256,256]{1,2,0:T(8,128)}, u32[]{:S(2)}) copy-start(f32[2,256,256]{1,2,0:T(8,128)} %copy.81) | copy-start | bytes 1572868
  125.8 24.2 %copy-start.13 = (f32[2,256,256]{1,2,0:T(8,128)S(1)}, f32[2,256,256]{1,2,0:T(8,128)}, u32[]{:S(2)}) copy-start(f32[2,256,256]{1,2,0:T(8,128)} %copy.84) | copy-start | bytes 1572868
  125.9 24.2 %copy-start.23 = (f32[4,256,256]{1,2,0:T(8,128)S(1)}, f32[4,256,256]{1,2,0:T(8,128)}, u32[]{:S(2)}) copy-start(f32[4,256,256]{1,2,0:T(8,128)} %get-tuple-element.65) | copy-start | bytes 3145732
  125.9 15.8 %collective-permute-start.5 = (f32[3,128,384]{1,2,0:T(8,128)S(1)}, f32[3,128,384]{1,2,0:T(8,128)S(1)}, u32[]{:S(2)}, u32[]{:S(2)}) collective-permute-start(f32[3,128,384]{1,2,0:T(8,128)S(1)} %get-tuple-element.83), channel_id=1, source_target_pairs={{16,0},{32,16},{48,32},{64,48},{80,64},{96,80},{112,96},{128,112},... | collective-permute-start | bytes 1769480 | tf_op jit(solution)/shard_map/ppermute | solution.py:26
  143.2 16.2 %collective-permute-start.6 = (f32[3,640,128]{1,2,0:T(8,128)}, f32[3,640,128]{1,2,0:T(8,128)}, u32[]{:S(2)}, u32[]{:S(2)}) collective-permute-start(f32[3,640,128]{1,2,0:T(8,128)} %get-tuple-element.74), channel_id=1, source_target_pairs={{0,1},{1,2},{2,3},{3,4},{4,5},{5,6},{6,7},{7,8},{8,9},{9,10},{10,1... | collective-permute-start | bytes 2949128 | tf_op jit(solution)/shard_map/ppermute | solution.py:24
  148.1 15.7 %collective-permute-start.7 = (f32[3,640,128]{1,2,0:T(8,128)}, f32[3,640,128]{1,2,0:T(8,128)}, u32[]{:S(2)}, u32[]{:S(2)}) collective-permute-start(f32[3,640,128]{1,2,0:T(8,128)} %get-tuple-element.75), channel_id=1, source_target_pairs={{1,0},{2,1},{3,2},{4,3},{5,4},{6,5},{7,6},{8,7},{9,8},{10,9},{11,1... | collective-permute-start | bytes 2949128 | tf_op jit(solution)/shard_map/ppermute | solution.py:26
  152.8 360.0 %all-reduce.11.cloned.1.call-start = ((), (), s32[]{:S(2)}) async-start(), calls=%async_computation.1 | async-start | bytes 2621440 | tf_op jit(solution)/shard_map/psum | solution.py:148
  165.4 7.4 collective-permute-start.8
  170.8 6.6 collective-permute-start.9
  177.5 142.8 %collective-permute-start.10 = (f32[2,384,128]{1,2,0:T(8,128)S(1)}, f32[2,384,128]{1,2,0:T(8,128)S(1)}, u32[]{:S(2)}, u32[]{:S(2)}) collective-permute-start(f32[2,384,128]{1,2,0:T(8,128)S(1)} %pad_maximum_fusion.14), channel_id=1, source_target_pairs={{0,1},{1,2},{2,3},{3,4},{4,5},{5,6},{6,7},{7,8},{8,9},{9,10},{10,1... | collective-permute-start | bytes 1179656 | tf_op jit(solution)/shard_map/ppermute | solution.py:24
  181.2 139.1 %collective-permute-start.11 = (f32[2,384,128]{1,2,0:T(8,128)S(1)}, f32[2,384,128]{1,2,0:T(8,128)S(1)}, u32[]{:S(2)}, u32[]{:S(2)}) collective-permute-start(f32[2,384,128]{1,2,0:T(8,128)S(1)} %pad_maximum_fusion.14), channel_id=1, source_target_pairs={{1,0},{2,1},{3,2},{4,3},{5,4},{6,5},{7,6},{8,7},{9,8},{10,9},{11,1... | collective-permute-start | bytes 1179656 | tf_op jit(solution)/shard_map/ppermute | solution.py:26
  320.2 396.8 %all-reduce.13.cloned.1.call-start = ((), (), s32[]{:S(2)}) async-start(), calls=%async_computation.2 | async-start | bytes 2621440 | tf_op jit(solution)/shard_map/psum | solution.py:148
  327.7 187.0 %copy-start.22 = (f32[2,2,256,256]{2,3,1,0:T(8,128)S(1)}, f32[2,2,256,256]{2,3,1,0:T(8,128)}, u32[]{:S(2)}) copy-start(f32[2,2,256,256]{2,3,1,0:T(8,128)} %copy.102) | copy-start | bytes 3145732
  558.9 350.5 %all-reduce.9.cloned.1.call-start = ((), (), s32[]{:S(2)}) async-start(), calls=%async_computation | async-start | bytes 2621440 | tf_op jit(solution)/shard_map/psum | solution.py:148
  583.6 19.5 %collective-permute-start.12 = (f32[3,128,384]{1,2,0:T(8,128)S(1)}, f32[3,128,384]{1,2,0:T(8,128)S(1)}, u32[]{:S(2)}, u32[]{:S(2)}) collective-permute-start(f32[3,128,384]{1,2,0:T(8,128)S(1)} %get-tuple-element.80), channel_id=1, source_target_pairs={{0,16},{16,32},{32,48},{48,64},{64,80},{80,96},{96,112},{112,128},... | collective-permute-start | bytes 1769480 | tf_op jit(solution)/shard_map/ppermute | solution.py:24
  587.2 21.2 %collective-permute-start.13 = (f32[3,128,384]{1,2,0:T(8,128)S(1)}, f32[3,128,384]{1,2,0:T(8,128)S(1)}, u32[]{:S(2)}, u32[]{:S(2)}) collective-permute-start(f32[3,128,384]{1,2,0:T(8,128)S(1)} %get-tuple-element.81), channel_id=1, source_target_pairs={{16,0},{32,16},{48,32},{64,48},{80,64},{96,80},{112,96},{128,112},... | collective-permute-start | bytes 1769480 | tf_op jit(solution)/shard_map/ppermute | solution.py:26
  609.9 107.2 %collective-permute-start.14 = (f32[3,640,128]{1,2,0:T(8,128)}, f32[3,640,128]{1,2,0:T(8,128)}, u32[]{:S(2)}, u32[]{:S(2)}) collective-permute-start(f32[3,640,128]{1,2,0:T(8,128)} %get-tuple-element.72), channel_id=1, source_target_pairs={{0,1},{1,2},{2,3},{3,4},{4,5},{5,6},{6,7},{7,8},{8,9},{9,10},{10,1... | collective-permute-start | bytes 2949128 | tf_op jit(solution)/shard_map/ppermute | solution.py:24
  611.8 105.3 %collective-permute-start.15 = (f32[3,640,128]{1,2,0:T(8,128)}, f32[3,640,128]{1,2,0:T(8,128)}, u32[]{:S(2)}, u32[]{:S(2)}) collective-permute-start(f32[3,640,128]{1,2,0:T(8,128)} %get-tuple-element.73), channel_id=1, source_target_pairs={{1,0},{2,1},{3,2},{4,3},{5,4},{6,5},{7,6},{8,7},{9,8},{10,9},{11,1... | collective-permute-start | bytes 2949128 | tf_op jit(solution)/shard_map/ppermute | solution.py:26
  (30 other events, 123.9 us)
Sparse Core Ops, SparseCore 0:
  152.9 167.2 all-reduce.14
  322.9 189.8 all-reduce.10
  559.0 157.9 all-reduce.12
  719.6 189.7 all-reduce.8
